TPU v7x, 512 devices: a whole 4x8x8 slice. The times are simulated.
512 devices in a mesh: dp: 32 (over y_lo, z), row: 4 (over x), col: 4 (over y_hi, core).
Axes of the slice: x: 4, y: 8 (y_hi: 2, y_lo: 4; y = y_hi * 4 + y_lo), z: 8, core: 2. Of those that a mesh axis runs over, the one named last changes fastest.
Arguments:
- query_out: bfloat16 [6144, 4096], P(('dp', 'row'), 'col'), may hold values from -6 to 6
- query_in: bfloat16 [6144, 4096], P(('dp', 'col')), may hold values from -6 to 6
- out_basis: bfloat16 [4096, 4096], P('col', ('dp', 'row')), may hold values from -0.09375 to 0.09375
- in_basis: bfloat16 [4096, 4096], P(('dp', 'row'), 'col'), may hold values from -0.09375 to 0.09375
- eigvals: float32 [4096, 4096], P(('dp', 'row'), 'col'), may hold values from 16 to 1024
- train_out: bfloat16 [6144, 4096], P(('dp', 'row'), 'col'), may hold values from -0.09375 to 0.09375
- train_in: bfloat16 [6144, 4096], P(('dp', 'col')), may hold values from -0.09375 to 0.09375
Outputs:
- precond: float32 [4096, 4096], P(('dp', 'row'), 'col')
- scores: float32 [6144], P('dp')
All inputs are finite; a program needn't handle non-finite values.
Results may differ from a plain program's by a relative error of at most 0.028.
Values may be sent and summed in bfloat16 or wider, within the bound.
No kernel may reach another device: no remote copies, remote signals or barrier semaphores. Data moves between devices by JAX's collectives and lax.ppermute only.
A program may use at most 64 MiB of HBM per device.

v0:
```python
import jax
import jax.numpy as jnp
from jax import lax
from jax.sharding import PartitionSpec as P

damping = 1.0


def rotate_out(tok_rows, basis_panel):
    gathered = lax.all_gather(tok_rows, "row", axis=0, tiled=True)
    partial_sum = jnp.dot(gathered, basis_panel, preferred_element_type=jnp.float32)
    return lax.psum(partial_sum.astype(jnp.bfloat16), "col")


def rotate_in(tok_rows, basis_panel):
    groups = lax.axis_size("dp")
    row_count = lax.axis_size("row")
    sub_width = tok_rows.shape[1] // (groups * row_count)
    split_rows = tok_rows.reshape(tok_rows.shape[0], groups, row_count, sub_width)
    picked = lax.dynamic_index_in_dim(split_rows, lax.axis_index("row"), 2, keepdims=False)
    picked = picked.reshape(tok_rows.shape[0], groups * sub_width)
    gathered = lax.all_gather(picked, "col", axis=0, tiled=True)
    partial_sum = jnp.dot(gathered, basis_panel, preferred_element_type=jnp.float32)
    return lax.psum(partial_sum.astype(jnp.bfloat16), "row")


def per_device(query_out, query_in, out_basis, in_basis, eigvals, train_out, train_in):
    panel_out = lax.all_gather(out_basis, "dp", axis=1, tiled=True)
    panel_in = lax.all_gather(in_basis, "dp", axis=0, tiled=True)
    query_rot = rotate_out(query_out, panel_out)
    query_inr = rotate_in(query_in, panel_in)
    partial_grad = lax.dot_general(
        query_rot, query_inr, (((0,), (0,)), ((), ())), preferred_element_type=jnp.float32
    )
    rows_own = eigvals.shape[0]
    summed = lax.psum(partial_grad.astype(jnp.bfloat16), "dp").astype(jnp.float32)
    owned = lax.dynamic_slice_in_dim(summed, lax.axis_index("dp") * rows_own, rows_own, 0)
    precond = owned / (eigvals + damping)
    shared = precond.astype(jnp.bfloat16)
    train_rot = rotate_out(train_out, panel_out)
    train_inr = rotate_in(train_in, panel_in)
    mixed = jnp.dot(
        train_rot,
        lax.all_gather(shared, "dp", axis=0, tiled=True),
        preferred_element_type=jnp.float32,
    )
    partial_scores = jnp.sum(mixed * train_inr.astype(jnp.float32), axis=1)
    scores = lax.psum(partial_scores, ("row", "col"))
    return (precond, scores)


def solution(mesh):
    in_specs = (
        P(("dp", "row"), "col"),
        P(("dp", "col"), None),
        P("col", ("dp", "row")),
        P(("dp", "row"), "col"),
        P(("dp", "row"), "col"),
        P(("dp", "row"), "col"),
        P(("dp", "col"), None),
    )
    out_specs = (P(("dp", "row"), "col"), P("dp"))
    return jax.shard_map(
        per_device, mesh=mesh, in_specs=in_specs, out_specs=out_specs, check_vma=False
    )
```

profile of v0, /device:TPU:1, one launch (start us, length us, event | category | flops | bytes accessed | tf_op | source)
XLA Modules:
  0.0 969.9 jit_solution(9535577205798143316)
XLA Ops:
  7.2 0.0 all-gather.6.cloned.1.call-start
  7.2 0.7 all-gather.6.cloned.1.call-update
  7.9 0.0 all-gather.4.cloned.1.call-start
  7.9 0.7 all-gather.4.cloned.1.call-update
  8.6 0.0 all-reduce.10.cloned.1.call-start
  8.7 1.5 copy.9
  10.2 1.5 copy.11
  11.7 0.1 copy.14
  11.8 0.1 copy.13
  12.0 16.7 %all_gather.27 = bf16[192,1024]{1,0:T(8,128)(2,1)S(1)} all-gather(bf16[48,1024]{1,0:T(8,128)(2,1)S(1)} %copy.14), channel_id=1, replica_groups=mesh['dp'=32,'row'=4,'col'=4] {'col'}, dimensions={0}, use_global_device_ids=true | all-gather | bytes 491520 | tf_op jit(solution)/shard_map/all_gather | solution.py:22
  28.7 12.9 %all_gather.23 = bf16[192,1024]{1,0:T(8,128)(2,1)S(1)} all-gather(bf16[48,1024]{1,0:T(8,128)(2,1)S(1)} %copy.13), channel_id=1, replica_groups=mesh['dp'=32,'row'=4,'col'=4] {'col'}, dimensions={0}, use_global_device_ids=true | all-gather | bytes 491520 | tf_op jit(solution)/shard_map/all_gather | solution.py:22
  41.6 106.6 %all-gather.6.cloned.1.call-done = bf16[1024,1024]{1,0:T(8,128)(2,1)} async-done(((bf16[32,1024]{1,0:T(8,128)(2,1)}), bf16[1024,1024]{1,0:T(8,128)(2,1)}) %all-gather.6.cloned.1.call-update) | async-done | bytes 2097168 | tf_op jit(solution)/shard_map/all_gather | solution.py:29
  148.2 3.1 convolution_convert_fusion.1
  151.3 1.4 convolution_convert_fusion.3
  152.7 0.0 all-reduce.10.cloned.1.call-update
  152.7 0.0 all-reduce.8.cloned.1.call-start
  152.8 10.9 %all_gather.25 = bf16[192,1024]{1,0:T(8,128)(2,1)S(1)} all-gather(bf16[48,1024]{1,0:T(8,128)(2,1)S(1)} %copy-done.3), channel_id=1, replica_groups=mesh['dp'=32,'row'=4,'col'=4] {'row'}, dimensions={0}, use_global_device_ids=true | all-gather | bytes 491520 | tf_op jit(solution)/shard_map/all_gather | solution.py:10
  163.6 10.0 %all_gather.21 = bf16[192,1024]{1,0:T(8,128)(2,1)S(1)} all-gather(bf16[48,1024]{1,0:T(8,128)(2,1)S(1)} %copy-done.4), channel_id=1, replica_groups=mesh['dp'=32,'row'=4,'col'=4] {'row'}, dimensions={0}, use_global_device_ids=true | all-gather | bytes 491520 | tf_op jit(solution)/shard_map/all_gather | solution.py:10
  173.6 126.9 %all-gather.4.cloned.1.call-done = bf16[1024,1024]{0,1:T(8,128)(2,1)} async-done(((bf16[1024,32]{0,1:T(8,128)(2,1)}), bf16[1024,1024]{0,1:T(8,128)(2,1)}) %all-gather.4.cloned.1.call-update) | async-done | bytes 2097168 | tf_op jit(solution)/shard_map/all_gather | solution.py:28
  300.6 3.3 convolution_convert_fusion.2
  303.9 1.6 convolution_convert_fusion.4
  305.5 0.0 all-reduce.8.cloned.1.call-update
  305.5 0.0 all-reduce.6.cloned.1.call-start
  305.6 68.1 %all-reduce.10.cloned.1.call-done = (bf16[192,1024]{1,0:T(8,128)(2,1)}, bf16[192,1024]{1,0:T(8,128)(2,1)}) async-done(((bf16[192,1024]{1,0:T(8,128)(2,1)}, bf16[192,1024]{1,0:T(8,128)(2,1)}), (bf16[192,1024]{1,0:T(8,128)(2,1)}, bf16[192,1024]{1,0:T(8,128)(2,1)})) %all-reduce.10.cloned.1.call-update) | async-done | bytes 786448 | tf_op jit(solution)/shard_map/psum | solution.py:24
  373.7 75.0 %all-reduce.8.cloned.1.call-done = (bf16[192,1024]{1,0:T(8,128)(2,1)}, bf16[192,1024]{1,0:T(8,128)(2,1)}) async-done(((bf16[192,1024]{1,0:T(8,128)(2,1)}, bf16[192,1024]{1,0:T(8,128)(2,1)}), (bf16[192,1024]{1,0:T(8,128)(2,1)}, bf16[192,1024]{1,0:T(8,128)(2,1)})) %all-reduce.8.cloned.1.call-update) | async-done | bytes 786448 | tf_op jit(solution)/shard_map/psum | solution.py:12
  448.7 3.3 convolution_convert_fusion
  452.0 0.0 all-gather.8.cloned.1.call-start
  452.0 290.8 %all-reduce.6.cloned.1.call-done = bf16[1024,1024]{1,0:T(8,128)(2,1)} async-done(((bf16[1024,1024]{1,0:T(8,128)(2,1)}), bf16[1024,1024]{1,0:T(8,128)(2,1)}) %all-reduce.6.cloned.1.call-update) | async-done | bytes 2097168 | tf_op jit(solution)/shard_map/psum | solution.py:36
  742.8 1.5 fusion.1
  744.4 150.6 %all-gather.8.cloned.1.call-done = bf16[1024,1024]{1,0:T(8,128)(2,1)} async-done(((bf16[32,1024]{1,0:T(8,128)(2,1)}), bf16[1024,1024]{1,0:T(8,128)(2,1)}) %all-gather.8.cloned.1.call-update) | async-done | bytes 2097168 | tf_op jit(solution)/shard_map/all_gather | solution.py:44
  895.0 2.3 fusion
  897.2 65.8 %psum.47 = f32[192]{0:T(256)} all-reduce(f32[192]{0:T(256)S(1)} %fusion), channel_id=1, replica_groups=mesh['dp'=32,'row'=4,'col'=4] {'row','col'}, use_global_device_ids=true, to_apply=%region_6.7 | all-reduce | flops 192 | bytes 1536 | tf_op jit(solution)/shard_map/psum | solution.py:48
  (17 shorter events, 0.1 us)
Async XLA Ops:
  7.2 141.1 %all-gather.6.cloned.1.call-start = ((), (), s32[]{:S(2)}) async-start(), calls=%async_computation.1 | async-start | bytes 2162688 | tf_op jit(solution)/shard_map/all_gather | solution.py:29
  7.9 292.7 %all-gather.4.cloned.1.call-start = ((), (), s32[]{:S(2)}) async-start(), calls=%async_computation | async-start | bytes 2162688 | tf_op jit(solution)/shard_map/all_gather | solution.py:28
  8.6 365.1 %all-reduce.10.cloned.1.call-start = ((), (), s32[]{:S(2)}) async-start(), calls=%async_computation.5 | async-start | bytes 1572864 | tf_op jit(solution)/shard_map/psum | solution.py:24
  148.2 3.1 copy-start.1
  151.3 1.4 copy-start.3
  151.3 12.3 %copy-start.4 = (bf16[48,1024]{1,0:T(8,128)(2,1)S(1)}, bf16[48,1024]{1,0:T(8,128)(2,1)}, u32[]{:S(2)}) copy-start(bf16[48,1024]{1,0:T(8,128)(2,1)} %param.7) | copy-start | bytes 294916
  152.7 295.9 %all-reduce.8.cloned.1.call-start = ((), (), s32[]{:S(2)}) async-start(), calls=%async_computation.4 | async-start | bytes 1572864 | tf_op jit(solution)/shard_map/psum | solution.py:12
  300.6 3.3 copy-start
  305.5 437.3 %all-reduce.6.cloned.1.call-start = ((), (), s32[]{:S(2)}) async-start(), calls=%async_computation.2 | async-start | bytes 4194304 | tf_op jit(solution)/shard_map/psum | solution.py:36
  448.7 294.2 %copy-start.2 = (f32[32,1024]{1,0:T(8,128)S(1)}, f32[32,1024]{1,0:T(8,128)}, u32[]{:S(2)}) copy-start(f32[32,1024]{1,0:T(8,128)} %param.11) | copy-start | bytes 393220
  448.7 446.3 %copy-start.5 = (bf16[192,1024]{1,0:T(8,128)(2,1)S(1)}, bf16[192,1024]{1,0:T(8,128)(2,1)}, u32[]{:S(2)}) copy-start(bf16[192,1024]{1,0:T(8,128)(2,1)} %get-tuple-element.5) | copy-start | bytes 1179652
  448.7 446.3 %copy-start.6 = (bf16[192,1024]{1,0:T(8,128)(2,1)S(1)}, bf16[192,1024]{1,0:T(8,128)(2,1)}, u32[]{:S(2)}) copy-start(bf16[192,1024]{1,0:T(8,128)(2,1)} %get-tuple-element.3) | copy-start | bytes 1179652
  452.0 443.0 %all-gather.8.cloned.1.call-start = ((), (), s32[]{:S(2)}) async-start(), calls=%async_computation.3 | async-start | bytes 2162688 | tf_op jit(solution)/shard_map/all_gather | solution.py:44
Sparse Core Ops, SparseCore 0:
  10.0 138.1 all-gather.5
  150.3 150.2 all-gather.3
  303.0 70.6 all-reduce.9
  376.6 72.0 all-reduce.7
  452.1 290.6 all-reduce.5
  744.7 150.1 all-gather.7
where the time goes:
time: 970 us
  waiting for transfers between devices  819 us (84%)
  blocking collectives  116 us (12%)
  matrix products  14.9 us (2%)
  between operations  14.2 us (1%)
    psum x1, waiting for transfers between devices, per_device(): lax.psum(partial_grad.astype(jnp.bfloat16), 'dp').astype(jnp.float32)  291 us
    all_gather x1, waiting for transfers between devices, per_device(): lax.all_gather(shared, 'dp', axis=0, tiled=True)  151 us
    all_gather x1, waiting for transfers between devices, per_device(): panel_out = lax.all_gather(out_basis, 'dp', axis=1, tiled=True)  127 us
    all_gather x1, waiting for transfers between devices, per_device(): panel_in = lax.all_gather(in_basis, 'dp', axis=0, tiled=True)  107 us
    psum x1, waiting for transfers between devices, rotate_out(): return lax.psum(partial_sum.astype(jnp.bfloat16), 'col')  75 us
    psum x1, waiting for transfers between devices, rotate_in(): return lax.psum(partial_sum.astype(jnp.bfloat16), 'row')  68.1 us
    psum x1, blocking collectives, per_device(): scores = lax.psum(partial_scores, ('row', 'col'))  65.8 us
    all_gather x2, blocking collectives, rotate_in(): gathered = lax.all_gather(picked, 'col', axis=0, tiled=True)  29.6 us
  transfers between devices with their start and end apart: 6, of which 6 were waited for; matrix products, arithmetic and copies ran while one was open for 1% of the time, Pallas kernels for 0%

commit v1 on v0

--- a/solution.py
+++ b/solution.py
@@ -6,8 +6,26 @@
 damping = 1.0
 
 
+def collect(array, axis, dim):
+    ways, here, lap = (lax.axis_size(axis), lax.axis_index(axis), array.shape[dim])
+    shape = [n * ways if d == dim else n for d, n in enumerate(array.shape)]
+    full = lax.dynamic_update_slice_in_dim(
+        jnp.zeros(shape, array.dtype), array, here * lap, axis=dim
+    )
+    going_up = going_down = array
+    for far in range(1, ways // 2 + 1):
+        going_up = lax.ppermute(going_up, axis, [(d, (d + 1) % ways) for d in range(ways)])
+        full = lax.dynamic_update_slice_in_dim(full, going_up, (here - far) % ways * lap, axis=dim)
+        if 2 * far < ways:
+            going_down = lax.ppermute(going_down, axis, [(d, (d - 1) % ways) for d in range(ways)])
+            full = lax.dynamic_update_slice_in_dim(
+                full, going_down, (here + far) % ways * lap, axis=dim
+            )
+    return full
+
+
 def rotate_out(tok_rows, basis_panel):
-    gathered = lax.all_gather(tok_rows, "row", axis=0, tiled=True)
+    gathered = collect(tok_rows, "row", 0)
     partial_sum = jnp.dot(gathered, basis_panel, preferred_element_type=jnp.float32)
     return lax.psum(partial_sum.astype(jnp.bfloat16), "col")
 

time: 970 us -> 971 us (level)
  starting transfers between devices: 0.24 us -> 17.9 us
  waiting for transfers between devices: 819 us -> 809 us
    all_gather x2 -> x0, blocking collectives: 20.9 us -> none  [rotate_out(): gathered = lax.all_gather(tok_rows, 'row', axis=0, tiled=True)]
    ppermute x0 -> x6, starting transfers between devices: none -> 17.6 us  [the longest x4 10 us: collect(): lax.ppermute(going_up, axis, [(d, (d + 1) % ways) for d in range(ways)])]
    all_gather x2, blocking collectives: 29.6 us -> 44.2 us  [rotate_in(): gathered = lax.all_gather(picked, 'col', axis=0, tiled=True)]
    psum x1, waiting for transfers between devices: 68.1 us -> 53.7 us  [rotate_in(): return lax.psum(partial_sum.astype(jnp.bfloat16), 'row')]
    all_gather x1, waiting for transfers between devices: 127 us -> 114 us  [per_device(): panel_out = lax.all_gather(out_basis, 'dp', axis=1, tiled=True)]
    psum x1, waiting for transfers between devices: 75 us -> 84.8 us  [rotate_out(): return lax.psum(partial_sum.astype(jnp.bfloat16), 'col')]
  transfers between devices with their start and end apart: 6 -> 12, of which waited for: 6 -> 8; matrix products, arithmetic and copies ran while one was open for 1% -> 1% of each run, Pallas kernels for 0% -> 0%
where the time goes in v1:
time: 971 us
  waiting for transfers between devices  809 us (83%)
  blocking collectives  110 us (11%)
  starting transfers between devices  17.9 us (2%)
  matrix products  14.9 us (2%)
  between operations  14.4 us (1%)
    psum x1, waiting for transfers between devices, per_device(): lax.psum(partial_grad.astype(jnp.bfloat16), 'dp').astype(jnp.float32)  295 us
    all_gather x1, waiting for transfers between devices, per_device(): lax.all_gather(shared, 'dp', axis=0, tiled=True)  151 us
    all_gather x1, waiting for transfers between devices, per_device(): panel_out = lax.all_gather(out_basis, 'dp', axis=1, tiled=True)  114 us
    all_gather x1, waiting for transfers between devices, per_device(): panel_in = lax.all_gather(in_basis, 'dp', axis=0, tiled=True)  105 us
    psum x1, waiting for transfers between devices, rotate_out(): return lax.psum(partial_sum.astype(jnp.bfloat16), 'col')  84.8 us
    psum x1, blocking collectives, per_device(): scores = lax.psum(partial_scores, ('row', 'col'))  65.8 us
    psum x1, waiting for transfers between devices, rotate_in(): return lax.psum(partial_sum.astype(jnp.bfloat16), 'row')  53.7 us
    all_gather x2, blocking collectives, rotate_in(): gathered = lax.all_gather(picked, 'col', axis=0, tiled=True)  44.2 us
  transfers between devices with their start and end apart: 12, of which 8 were waited for; matrix products, arithmetic and copies ran while one was open for 1% of the time, Pallas kernels for 0%

profile of v1, /device:TPU:1, one launch (start us, length us, event | category | flops | bytes accessed | tf_op | source)
XLA Modules:
  0.0 971.0 jit_solution(11326834924682512442)
XLA Ops:
  7.2 0.7 all-gather.4.cloned.1.call-update
  7.9 0.7 all-gather.6.cloned.1.call-update
  8.7 3.9 collective-permute-start.3
  12.6 3.2 collective-permute-start.4
  15.8 2.1 collective-permute-start
  17.9 4.4 collective-permute-start.1
  22.4 1.5 copy.9
  23.9 1.5 copy.11
  25.5 0.1 copy.14
  25.8 1.9 collective-permute-start.5
  27.8 2.1 collective-permute-start.2
  30.0 2.4 collective-permute-done.5
  32.4 1.9 collective-permute-done.2
  34.3 113.8 %all-gather.4.cloned.1.call-done = bf16[1024,1024]{0,1:T(8,128)(2,1)} async-done(((bf16[1024,32]{0,1:T(8,128)(2,1)}), bf16[1024,1024]{0,1:T(8,128)(2,1)}) %all-gather.4.cloned.1.call-update) | async-done | bytes 2097168 | tf_op jit(solution)/shard_map/all_gather | solution.py:46
  148.2 3.4 convolution_convert_fusion.2
  151.5 1.6 convolution_convert_fusion.4
  153.3 33.0 %all_gather.19 = bf16[192,1024]{1,0:T(8,128)(2,1)S(1)} all-gather(bf16[48,1024]{1,0:T(8,128)(2,1)S(1)} %copy.14), channel_id=1, replica_groups=mesh['dp'=32,'row'=4,'col'=4] {'col'}, dimensions={0}, use_global_device_ids=true | all-gather | bytes 491520 | tf_op jit(solution)/shard_map/all_gather | solution.py:40
  186.3 0.1 copy.13
  186.4 11.2 %all_gather.16 = bf16[192,1024]{1,0:T(8,128)(2,1)S(1)} all-gather(bf16[48,1024]{1,0:T(8,128)(2,1)S(1)} %copy.13), channel_id=1, replica_groups=mesh['dp'=32,'row'=4,'col'=4] {'col'}, dimensions={0}, use_global_device_ids=true | all-gather | bytes 491520 | tf_op jit(solution)/shard_map/all_gather | solution.py:40
  197.6 104.6 %all-gather.6.cloned.1.call-done = bf16[1024,1024]{1,0:T(8,128)(2,1)} async-done(((bf16[32,1024]{1,0:T(8,128)(2,1)}), bf16[1024,1024]{1,0:T(8,128)(2,1)}) %all-gather.6.cloned.1.call-update) | async-done | bytes 2097168 | tf_op jit(solution)/shard_map/all_gather | solution.py:47
  302.2 3.1 convolution_convert_fusion.1
  305.3 1.3 convolution_convert_fusion.3
  306.7 0.0 all-reduce.6.cloned.1.call-start
  306.7 84.8 %all-reduce.8.cloned.1.call-done = (bf16[192,1024]{1,0:T(8,128)(2,1)}, bf16[192,1024]{1,0:T(8,128)(2,1)}) async-done(((bf16[192,1024]{1,0:T(8,128)(2,1)}, bf16[192,1024]{1,0:T(8,128)(2,1)}), (bf16[192,1024]{1,0:T(8,128)(2,1)}, bf16[192,1024]{1,0:T(8,128)(2,1)})) %all-reduce.8.cloned.1.call-update) | async-done | bytes 786448 | tf_op jit(solution)/shard_map/psum | solution.py:30
  391.5 53.7 %all-reduce.10.cloned.1.call-done = (bf16[192,1024]{1,0:T(8,128)(2,1)}, bf16[192,1024]{1,0:T(8,128)(2,1)}) async-done(((bf16[192,1024]{1,0:T(8,128)(2,1)}, bf16[192,1024]{1,0:T(8,128)(2,1)}), (bf16[192,1024]{1,0:T(8,128)(2,1)}, bf16[192,1024]{1,0:T(8,128)(2,1)})) %all-reduce.10.cloned.1.call-update) | async-done | bytes 786448 | tf_op jit(solution)/shard_map/psum | solution.py:42
  445.2 3.3 convolution_convert_fusion
  448.5 0.0 all-gather.8.cloned.1.call-start
  448.6 295.3 %all-reduce.6.cloned.1.call-done = bf16[1024,1024]{1,0:T(8,128)(2,1)} async-done(((bf16[1024,1024]{1,0:T(8,128)(2,1)}), bf16[1024,1024]{1,0:T(8,128)(2,1)}) %all-reduce.6.cloned.1.call-update) | async-done | bytes 2097168 | tf_op jit(solution)/shard_map/psum | solution.py:54
  743.9 1.5 fusion.1
  745.4 150.6 %all-gather.8.cloned.1.call-done = bf16[1024,1024]{1,0:T(8,128)(2,1)} async-done(((bf16[32,1024]{1,0:T(8,128)(2,1)}), bf16[1024,1024]{1,0:T(8,128)(2,1)}) %all-gather.8.cloned.1.call-update) | async-done | bytes 2097168 | tf_op jit(solution)/shard_map/all_gather | solution.py:62
  896.0 2.3 fusion
  898.3 65.8 %psum.47 = f32[192]{0:T(256)} all-reduce(f32[192]{0:T(256)S(1)} %fusion), channel_id=1, replica_groups=mesh['dp'=32,'row'=4,'col'=4] {'row','col'}, use_global_device_ids=true, to_apply=%region_6.7 | all-reduce | flops 192 | bytes 1536 | tf_op jit(solution)/shard_map/psum | solution.py:66
  (37 shorter events, 0.5 us)
Async XLA Ops:
  7.2 141.0 %all-gather.4.cloned.1.call-start = ((), (), s32[]{:S(2)}) async-start(), calls=%async_computation | async-start | bytes 2162688 | tf_op jit(solution)/shard_map/all_gather | solution.py:46
  7.9 294.3 %all-gather.6.cloned.1.call-start = ((), (), s32[]{:S(2)}) async-start(), calls=%async_computation.1 | async-start | bytes 2162688 | tf_op jit(solution)/shard_map/all_gather | solution.py:47
  8.6 382.8 %all-reduce.8.cloned.1.call-start = ((), (), s32[]{:S(2)}) async-start(), calls=%async_computation.4 | async-start | bytes 1572864 | tf_op jit(solution)/shard_map/psum | solution.py:30
  8.7 17.1 %collective-permute-start.3 = (bf16[48,1024]{1,0:T(8,128)(2,1)}, bf16[48,1024]{1,0:T(8,128)(2,1)S(1)}, u32[]{:S(2)}, u32[]{:S(2)}) collective-permute-start(bf16[48,1024]{1,0:T(8,128)(2,1)} %param.12), channel_id=1, source_target_pairs={{0,4},{4,8},{8,12},{12,0},{1,5},{5,9},{9,13},{13,1},{2,6},{6,10},{... | collective-permute-start | bytes 294920 | tf_op jit(solution)/shard_map/ppermute | solution.py:17
  12.6 17.3 %collective-permute-start.4 = (bf16[48,1024]{1,0:T(8,128)(2,1)}, bf16[48,1024]{1,0:T(8,128)(2,1)S(1)}, u32[]{:S(2)}, u32[]{:S(2)}) collective-permute-start(bf16[48,1024]{1,0:T(8,128)(2,1)} %param.12), channel_id=1, source_target_pairs={{0,12},{4,0},{8,4},{12,8},{1,13},{5,1},{9,5},{13,9},{2,14},{6,2},{... | collective-permute-start | bytes 294920 | tf_op jit(solution)/shard_map/ppermute | solution.py:20
  15.8 11.9 %collective-permute-start = (bf16[48,1024]{1,0:T(8,128)(2,1)}, bf16[48,1024]{1,0:T(8,128)(2,1)S(1)}, u32[]{:S(2)}, u32[]{:S(2)}) collective-permute-start(bf16[48,1024]{1,0:T(8,128)(2,1)} %param.7), channel_id=1, source_target_pairs={{0,4},{4,8},{8,12},{12,0},{1,5},{5,9},{9,13},{13,1},{2,6},{6,10},{... | collective-permute-start | bytes 294920 | tf_op jit(solution)/shard_map/ppermute | solution.py:17
  17.9 12.0 %collective-permute-start.1 = (bf16[48,1024]{1,0:T(8,128)(2,1)}, bf16[48,1024]{1,0:T(8,128)(2,1)S(1)}, u32[]{:S(2)}, u32[]{:S(2)}) collective-permute-start(bf16[48,1024]{1,0:T(8,128)(2,1)} %param.7), channel_id=1, source_target_pairs={{0,12},{4,0},{8,4},{12,8},{1,13},{5,1},{9,5},{13,9},{2,14},{6,2},{... | collective-permute-start | bytes 294920 | tf_op jit(solution)/shard_map/ppermute | solution.py:20
  22.4 3.3 copy-start.3
  23.9 1.8 copy-start.4
  25.8 6.6 collective-permute-start.5
  27.8 6.6 collective-permute-start.2
  148.2 3.4 copy-start.1
  153.2 292.0 %all-reduce.10.cloned.1.call-start = ((), (), s32[]{:S(2)}) async-start(), calls=%async_computation.5 | async-start | bytes 1572864 | tf_op jit(solution)/shard_map/psum | solution.py:42
  302.2 3.1 copy-start
  306.7 437.2 %all-reduce.6.cloned.1.call-start = ((), (), s32[]{:S(2)}) async-start(), calls=%async_computation.2 | async-start | bytes 4194304 | tf_op jit(solution)/shard_map/psum | solution.py:54
  445.2 298.6 %copy-start.2 = (f32[32,1024]{1,0:T(8,128)S(1)}, f32[32,1024]{1,0:T(8,128)}, u32[]{:S(2)}) copy-start(f32[32,1024]{1,0:T(8,128)} %param.11) | copy-start | bytes 393220
  445.2 450.8 %copy-start.5 = (bf16[192,1024]{1,0:T(8,128)(2,1)S(1)}, bf16[192,1024]{1,0:T(8,128)(2,1)}, u32[]{:S(2)}) copy-start(bf16[192,1024]{1,0:T(8,128)(2,1)} %get-tuple-element.3) | copy-start | bytes 1179652
  445.2 450.8 %copy-start.6 = (bf16[192,1024]{1,0:T(8,128)(2,1)S(1)}, bf16[192,1024]{1,0:T(8,128)(2,1)}, u32[]{:S(2)}) copy-start(bf16[192,1024]{1,0:T(8,128)(2,1)} %get-tuple-element.5) | copy-start | bytes 1179652
  448.5 447.5 %all-gather.8.cloned.1.call-start = ((), (), s32[]{:S(2)}) async-start(), calls=%async_computation.3 | async-start | bytes 2162688 | tf_op jit(solution)/shard_map/all_gather | solution.py:62
Sparse Core Ops, SparseCore 0:
  10.1 138.0 all-gather.3
  150.3 151.9 all-gather.5
  305.2 86.2 all-reduce.7
  393.7 51.4 all-reduce.9
  448.6 295.1 all-reduce.5
  745.8 150.1 all-gather.7
